TPU v7x, 256 devices: a whole 4x4x8 slice. The times are simulated.
256 devices in a mesh: row: 8 (over z), col: 32 (over x, y, core).
Axes of the slice: x: 4, y: 4, z: 8, core: 2. Of those that a mesh axis runs over, the one named last changes fastest.
Arguments:
- h_values: float32 [8, 512, 4096], P('row', 'col'), as said below
- h_places: int32 [8, 512], P('row', 'col'), may hold values from 0 to 15, as said below
- h_counts: int32 [8, 32], P('row', 'col'), may hold values from 0 to 16, as said below
- p_values: float32 [8, 512, 4096], P('row', 'col'), as said below
- p_places: int32 [8, 512], P('row', 'col'), may hold values from 0 to 15, as said below
- p_counts: int32 [8, 32], P('row', 'col'), may hold values from 0 to 16, as said below
- s_values: float32 [8, 512, 4096], P('row', 'col'), as said below
- s_places: int32 [8, 512], P('row', 'col'), may hold values from 0 to 15, as said below
- s_counts: int32 [8, 32], P('row', 'col'), may hold values from 0 to 16, as said below
- x_places: int32 [8, 512], P('row', 'col'), may hold values from 0 to 15, as said below
- x_counts: int32 [8, 32], P('row', 'col'), may hold values from 0 to 16, as said below
Outputs:
- gradient: float32 [8, 512, 4096], P('row', 'col')
Inputs may be any that keep to these rules, and one draw needn't show every extreme that they name: `h_places`: in each tile the 16 entries are a permutation of the tile's positions; the first count entries are the present blocks. Every pattern is symmetric, holds every block whose block row and block column lie in the same row panel, and every block (i, j) whose cyclic block distance min(|i - j|, 64 - |i - j|) is 2 or less or exactly 32. `p_places`: as for h_places. `s_places`: as for h_places. `x_places`: as for h_places. `h_counts`: every tile whose block columns lie in its own row panel is full. `p_counts`: as for h_counts. `s_counts`: as for h_counts. `x_counts`: as for h_counts. `h_values`: the assembled H is symmetric. `p_values`: the assembled P is symmetric. `s_values`: the assembled S is symmetric.
All inputs are finite; a program needn't handle non-finite values.
Results may differ from a plain program's by a relative error of at most 0.000088.
Values sent between devices are 32-bit elements; how exact they have to be, the bound alone decides.
A program may use at most 64 MiB of HBM per device.

v0:
```python
import jax
import jax.numpy as jnp
from jax import lax
from jax.sharding import PartitionSpec as P

BS = 64
TC = 2


def from_root(value, axis, source):
    kept = jnp.where(lax.axis_index(axis) == source, value, 0).astype(value.dtype)
    return lax.psum(kept, axis)


def assemble(values, places, counts):
    blocks_in = values[0]
    capacity = blocks_in.shape[0]
    slot_ids = lax.iota(jnp.int32, capacity)
    matches = (places[0][:, None] == slot_ids[None, :]) & (slot_ids[:, None] < counts[0, 0])
    spread = jnp.dot(matches.astype(jnp.float32).T, blocks_in, precision=lax.Precision.HIGHEST)
    row_count = capacity // TC
    return (
        spread.reshape(row_count, TC, BS, BS).transpose(0, 2, 1, 3).reshape(row_count * BS, TC * BS)
    )


def expand_mask(present, row_count, col_count):
    flags = present.reshape(row_count, col_count)
    return jnp.broadcast_to(flags[:, None, :, None], (row_count, BS, col_count, BS)).reshape(
        row_count * BS, col_count * BS
    )


def tile_mask(places, counts):
    capacity = places.shape[1]
    slot_ids = lax.iota(jnp.int32, capacity)
    matches = (places[0][:, None] == slot_ids[None, :]) & (slot_ids[:, None] < counts[0, 0])
    present = jnp.sum(matches.astype(jnp.float32), axis=0)
    return expand_mask(present, capacity // TC, TC)


def tile_to_slots(tile, places, counts):
    row_count = tile.shape[0] // BS
    blocks = (
        tile.reshape(row_count, BS, TC, BS).transpose(0, 2, 1, 3).reshape(row_count * TC, BS * BS)
    )
    picked = jnp.take(blocks, places[0], axis=0)
    slot_ids = lax.iota(jnp.int32, places.shape[1])
    used = (slot_ids < counts[0, 0]).astype(jnp.float32)
    return (picked * used[:, None])[None]


def shards(
    h_values,
    h_places,
    h_counts,
    p_values,
    p_places,
    p_counts,
    s_values,
    s_places,
    s_counts,
    x_places,
    x_counts,
):
    col_index = lax.axis_index("col")
    h_tile = assemble(h_values, h_places, h_counts)
    p_tile = assemble(p_values, p_places, p_counts)
    s_tile = assemble(s_values, s_places, s_counts)
    mask_tile = tile_mask(x_places, x_counts)
    row_width = h_tile.shape[0]
    col_width = h_tile.shape[1]
    p_columns, s_columns = (
        lax.all_gather(p_tile, "row", axis=0, tiled=True),
        lax.all_gather(s_tile, "row", axis=0, tiled=True),
    )
    product = jnp.dot(
        lax.all_gather(h_tile, "col", axis=1, tiled=True),
        p_columns,
        precision=lax.Precision.HIGHEST,
    )
    y_tile = mask_tile * product
    y_panel = lax.all_gather(y_tile, "col", axis=1, tiled=True)
    x_tile = mask_tile * jnp.dot(y_panel, s_columns, precision=lax.Precision.HIGHEST)
    per_panel = row_width // col_width
    source_row = col_index // per_panel
    offset = col_index % per_panel * col_width
    y_part = lax.dynamic_slice_in_dim(y_panel, offset, col_width, 0)
    y_mirror = from_root(y_part, "row", source_row)
    far_part = lax.dot_general(
        lax.all_gather(s_tile, "col", axis=1, tiled=True),
        y_mirror,
        (((1,), (1,)), ((), ())),
        precision=lax.Precision.HIGHEST,
    )
    mirrored = mask_tile * far_part
    return tile_to_slots(x_tile + mirrored, x_places, x_counts)


def solution(mesh):
    in_specs = (
        P("row", "col", None),
        P("row", "col"),
        P("row", "col"),
        P("row", "col", None),
        P("row", "col"),
        P("row", "col"),
        P("row", "col", None),
        P("row", "col"),
        P("row", "col"),
        P("row", "col"),
        P("row", "col"),
    )
    out_specs = P("row", "col", None)
    return jax.shard_map(shards, mesh=mesh, in_specs=in_specs, out_specs=out_specs, check_vma=False)
```

profile of v0, /device:TPU:2, one launch (start us, length us, event | category | flops | bytes accessed | tf_op | source)
XLA Modules:
  0.0 405.1 jit_solution(8840308818379448259)
XLA Ops:
  7.3 1.1 dot_general.34
  8.4 1.3 convolution_bitcast_fusion.1
  9.8 0.3 copy.26
  10.0 0.9 reshape.190
  11.9 0.7 convolution_bitcast_fusion.2
  12.8 0.9 reshape.189
  14.8 0.3 reshape.188
  15.2 40.0 %all-gather.8.cloned.1.call-done = f32[4096,128]{0,1:T(8,128)} async-done(((f32[512,128]{0,1:T(8,128)}), f32[4096,128]{0,1:T(8,128)}) %all-gather.8.cloned.1.call-update) | async-done | bytes 2097168 | tf_op jit(solution)/shard_map/all_gather | solution.py:74
  55.1 59.1 %all-gather.6.cloned.1.call-done = f32[512,4096]{0,1:T(8,128)} async-done(((f32[512,128]{0,1:T(8,128)}), f32[512,4096]{0,1:T(8,128)}) %all-gather.6.cloned.1.call-update) | async-done | bytes 8388624 | tf_op jit(solution)/shard_map/all_gather | solution.py:78
  114.2 16.5 %convolution_multiply_fusion = f32[512,128]{1,0:T(8,128)} fusion(f32[512,128]{1,0:T(8,128)S(1)} %reshape.188, f32[512,4096]{0,1:T(8,128)} %all-gather.6.cloned.1.call-done, f32[4096,128]{0,1:T(8,128)} %all-gather.8.cloned.1.call-done), kind=kOutput, calls=%fused_computation.7 | convolution fusion | flops 3221291008 | bytes 11010048 | tf_op jit(solution)/shard_map/dot_general | solution.py:77
  131.7 0.7 convolution_bitcast_fusion
  132.4 0.3 copy.28
  132.7 0.9 reshape.191
  133.6 0.5 all-gather.14.cloned.1.call-update
  134.4 60.4 %all-gather.10.cloned.1.call-done = f32[512,4096]{1,0:T(8,128)} async-done(((f32[512,128]{1,0:T(8,128)}), f32[512,4096]{1,0:T(8,128)}) %all-gather.10.cloned.1.call-update) | async-done | bytes 8388624 | tf_op jit(solution)/shard_map/all_gather | solution.py:83
  194.8 3.2 dynamic-slice_select_fusion
  198.0 39.7 %all-gather.12.cloned.1.call-done = f32[4096,128]{0,1:T(8,128)} async-done(((f32[512,128]{0,1:T(8,128)}), f32[4096,128]{0,1:T(8,128)}) %all-gather.12.cloned.1.call-update) | async-done | bytes 2097168 | tf_op jit(solution)/shard_map/all_gather | solution.py:75
  237.7 9.3 %fusion.29 = f32[512,128]{1,0:T(8,128)S(1)} fusion(f32[512,4096]{1,0:T(8,128)} %all-gather.10.cloned.1.call-done, f32[4096,128]{0,1:T(8,128)} %all-gather.12.cloned.1.call-done), kind=kOutput, calls=%fused_computation.48 | convolution fusion | flops 3221225472 | bytes 10747904 | tf_op jit(solution)/shard_map/dot_general | solution.py:84
  247.0 49.5 %all-gather.14.cloned.1.call-done = f32[512,4096]{0,1:T(8,128)} async-done(((f32[512,128]{0,1:T(8,128)}), f32[512,4096]{0,1:T(8,128)}) %all-gather.14.cloned.1.call-update) | async-done | bytes 8388624 | tf_op jit(solution)/shard_map/all_gather | solution.py:91
  296.6 83.7 %all-reduce.2.cloned.1.call-done = f32[128,4096]{1,0:T(8,128)} async-done(((f32[128,4096]{1,0:T(8,128)}), f32[128,4096]{1,0:T(8,128)}) %all-reduce.2.cloned.1.call-update) | async-done | bytes 2097168 | tf_op jit(solution)/shard_map/psum | solution.py:12
  380.3 16.0 %fusion = f32[512,128]{1,0:T(8,128)S(1)} fusion(f32[512,128]{1,0:T(8,128)S(1)} %reshape.188, f32[512,128]{1,0:T(8,128)S(1)} %fusion.29, f32[512,4096]{0,1:T(8,128)} %all-gather.14.cloned.1.call-done, f32[128,4096]{1,0:T(8,128)} %all-reduce.2.cloned.1.call-done), kind=kOutput, calls=%fused_computation.6 | convolution fusion | flops 3221356544 | bytes 11272192 | tf_op jit(solution)/shard_map/dot_general | solution.py:90
  396.3 0.3 reshape.192
  396.9 0.6 gather_fusion
  397.5 0.8 fusion.7
  (37 shorter events, 1.8 us)
Async XLA Ops:
  6.5 5.1 %copy-start = (f32[1,16,4096]{2,1,0:T(8,128)S(1)}, f32[1,16,4096]{2,1,0:T(8,128)}, u32[]{:S(2)}) copy-start(f32[1,16,4096]{2,1,0:T(8,128)} %param.11) | copy-start | bytes 786436
  6.5 48.6 %all-gather.8.cloned.1.call-start = ((), (), s32[]{:S(2)}) async-start(), calls=%async_computation.1 | async-start | bytes 2359296 | tf_op jit(solution)/shard_map/all_gather | solution.py:74
  8.4 3.5 copy-start.2
  10.9 3.5 copy-start.4
  10.9 103.3 %all-gather.6.cloned.1.call-start = ((), (), s32[]{:S(2)}) async-start(), calls=%async_computation | async-start | bytes 8650752 | tf_op jit(solution)/shard_map/all_gather | solution.py:78
  13.7 181.1 %all-gather.10.cloned.1.call-start = ((), (), s32[]{:S(2)}) async-start(), calls=%async_computation.2 | async-start | bytes 8650752 | tf_op jit(solution)/shard_map/all_gather | solution.py:83
  15.1 116.3 %copy-start.1 = (f32[1,16,4096]{2,1,0:T(8,128)S(1)}, f32[1,16,4096]{2,1,0:T(8,128)}, u32[]{:S(2)}) copy-start(f32[1,16,4096]{2,1,0:T(8,128)} %param.17) | copy-start | bytes 786436
  15.2 116.5 %copy-start.3 = (s32[1,16]{1,0:T(1,128)S(1)}, s32[1,16]{1,0:T(1,128)}, u32[]{:S(2)}) copy-start(s32[1,16]{1,0:T(1,128)} %param.18) | copy-start | bytes 196
  130.8 106.9 %all-gather.12.cloned.1.call-start = ((), (), s32[]{:S(2)}) async-start(), calls=%async_computation.3 | async-start | bytes 2359296 | tf_op jit(solution)/shard_map/all_gather | solution.py:75
  133.6 163.0 %all-gather.14.cloned.1.call-start = ((), (), s32[]{:S(2)}) async-start(), calls=%async_computation.4 | async-start | bytes 8650752 | tf_op jit(solution)/shard_map/all_gather | solution.py:91
  134.2 246.2 %all-reduce.2.cloned.1.call-start = ((), (), s32[]{:S(2)}) async-start(), calls=%async_computation.5 | async-start | bytes 4194304 | tf_op jit(solution)/shard_map/psum | solution.py:12
Sparse Core Ops, SparseCore 0:
  11.1 44.0 all-gather.7
  57.7 56.4 all-gather.5
  130.9 63.8 all-gather.9
  196.5 41.1 all-gather.11
  240.1 56.4 all-gather.13
  298.8 81.4 all-reduce.1
where the time goes:
time: 405 us
  waiting for transfers between devices  333 us (82%)
  matrix products  44.6 us (11%)
  between operations  16.4 us (4%)
  local copies, waits for them, and re-layouts  6.76 us (2%)
  other arithmetic  4.09 us (1%)
    psum x1, waiting for transfers between devices, from_root(): return lax.psum(kept, axis)  83.7 us
    all_gather x1, waiting for transfers between devices, shards(): y_panel = lax.all_gather(y_tile, 'col', axis=1, tiled=True)  60.4 us
    all_gather x1, waiting for transfers between devices, shards(): lax.all_gather(h_tile, 'col', axis=1, tiled=True)  59.1 us
    all_gather x1, waiting for transfers between devices, shards(): lax.all_gather(s_tile, 'col', axis=1, tiled=True)  49.5 us
    all_gather x1, waiting for transfers between devices, shards(): lax.all_gather(p_tile, 'row', axis=0, tiled=True)  40 us
    all_gather x1, waiting for transfers between devices, shards(): lax.all_gather(s_tile, 'row', axis=0, tiled=True)  39.7 us
    dot_general x1, matrix products, shards(): jnp.dot(lax.all_gather(h_tile, 'col', axis=1, tiled=True), p_columns, pre...  16.5 us
    dot_general x1, matrix products, shards(): lax.dot_general(lax.all_gather(s_tile, 'col', axis=1, tiled=True), y_mirr...  16 us
  transfers between devices with their start and end apart: 6, of which 6 were waited for; matrix products, arithmetic and copies ran while one was open for 4% of the time, Pallas kernels for 0%

commit v1 on v0

--- a/solution.py
+++ b/solution.py
@@ -5,6 +5,28 @@
 
 BS = 64
 TC = 2
+
+
+def in_order(tiles, dim):
+    tiles = jnp.moveaxis(tiles, 0, dim)
+    shape = tiles.shape
+    return tiles.reshape(*shape[:dim], shape[dim] * shape[dim + 1], *shape[dim + 2 :])
+
+
+def gather_around(x, axis, dim):
+    size = lax.axis_size(axis)
+    pairs = [(i, (i + 1) % size) for i in range(size)]
+    back = [(b, a) for a, b in pairs]
+    lower, upper = ([], [])
+    for step in range(size - 1):
+        if step % 2 == 0:
+            lower.append(lax.ppermute(lower[-1] if lower else x, axis, pairs))
+        else:
+            upper.append(lax.ppermute(upper[-1] if upper else x, axis, back))
+    blocks = jnp.stack([*lower[::-1], x, *upper])
+    shift = lax.axis_index(axis) - len(lower)
+    blocks = blocks[(jnp.arange(size) - shift) % size]
+    return in_order(blocks, dim)
 
 
 def from_root(value, axis, source):
@@ -71,7 +93,7 @@
     row_width = h_tile.shape[0]
     col_width = h_tile.shape[1]
     p_columns, s_columns = (
-        lax.all_gather(p_tile, "row", axis=0, tiled=True),
+        gather_around(p_tile, "row", 0),
         lax.all_gather(s_tile, "row", axis=0, tiled=True),
     )
     product = jnp.dot(

time: 405 us -> 363 us (0.90)
  waiting for transfers between devices: 333 us -> 269 us
  starting transfers between devices: 0.39 us -> 12.4 us
  local copies, waits for them, and re-layouts: 6.76 us -> 16.3 us
    all_gather x1, waiting for transfers between devices: 59.1 us -> 12.5 us  [shards(): lax.all_gather(h_tile, 'col', axis=1, tiled=True)]
    all_gather x1 -> x0, waiting for transfers between devices: 40 us -> none  [shards(): lax.all_gather(p_tile, 'row', axis=0, tiled=True)]
    ppermute x0 -> x7, waiting for transfers between devices: none -> 22.7 us  [the longest x4 22.7 us: gather_around(): lower.append(lax.ppermute(lower[-1] if lower else x, axis, pairs))]
    ppermute x0 -> x7, starting transfers between devices: none -> 12 us  [the longest x3 10 us: gather_around(): upper.append(lax.ppermute(upper[-1] if upper else x, axis, back))]
    unnamed x10 -> x17, local copies, waits for them, and re-layouts: 0.03 us -> 5.09 us
    gather x0 -> x2, local copies, waits for them, and re-layouts: none -> 4.33 us  [gather_around(): blocks = blocks[(jnp.arange(size) - shift) % size]]
  transfers between devices with their start and end apart: 6 -> 12, of which waited for: 6 -> 9; matrix products, arithmetic and copies ran while one was open for 4% -> 7% of each run, Pallas kernels for 0% -> 0%
where the time goes in v1:
time: 363 us
  waiting for transfers between devices  269 us (74%)
  matrix products  44.6 us (12%)
  local copies, waits for them, and re-layouts  16.3 us (4%)
  between operations  16.1 us (4%)
  starting transfers between devices  12.4 us (3%)
  other arithmetic  4.08 us (1%)
    psum x1, waiting for transfers between devices, from_root(): return lax.psum(kept, axis)  83.7 us
    all_gather x1, waiting for transfers between devices, shards(): y_panel = lax.all_gather(y_tile, 'col', axis=1, tiled=True)  60.3 us
    all_gather x1, waiting for transfers between devices, shards(): lax.all_gather(s_tile, 'col', axis=1, tiled=True)  49.6 us
    all_gather x1, waiting for transfers between devices, shards(): lax.all_gather(s_tile, 'row', axis=0, tiled=True)  39.8 us
    ppermute x4, waiting for transfers between devices, gather_around(): lower.append(lax.ppermute(lower[-1] if lower else x, axis, pairs))  22.7 us
    dot_general x1, matrix products, shards(): jnp.dot(lax.all_gather(h_tile, 'col', axis=1, tiled=True), p_columns, pre...  16.6 us
    dot_general x1, matrix products, shards(): lax.dot_general(lax.all_gather(s_tile, 'col', axis=1, tiled=True), y_mirr...  16 us
    all_gather x1, waiting for transfers between devices, shards(): lax.all_gather(h_tile, 'col', axis=1, tiled=True)  12.5 us
  transfers between devices with their start and end apart: 12, of which 9 were waited for; matrix products, arithmetic and copies ran while one was open for 7% of the time, Pallas kernels for 0%

profile of v1, /device:TPU:2, one launch (start us, length us, event | category | flops | bytes accessed | tf_op | source)
XLA Modules:
  0.0 362.8 jit_solution(16053600532998431220)
XLA Ops:
  6.5 1.2 dot_general.31
  8.4 1.3 convolution_bitcast_fusion.2
  10.0 0.9 reshape.241
  13.0 2.0 collective-permute-start
  15.0 10.2 %collective-permute-done = f32[512,128]{0,1:T(8,128)S(1)} collective-permute-done((f32[512,128]{0,1:T(8,128)S(1)}, f32[512,128]{0,1:T(8,128)S(1)}, u32[]{:S(2)}, u32[]{:S(2)}) %collective-permute-start) | collective-permute-done | bytes 262176 | tf_op jit(solution)/shard_map/ppermute | solution.py:23
  25.2 3.2 collective-permute-start.4
  28.5 5.5 %collective-permute-done.1 = f32[512,128]{0,1:T(8,128)S(1)} collective-permute-done((f32[512,128]{0,1:T(8,128)S(1)}, f32[512,128]{0,1:T(8,128)S(1)}, u32[]{:S(2)}, u32[]{:S(2)}) %collective-permute-start.1) | collective-permute-done | bytes 262176 | tf_op jit(solution)/shard_map/ppermute | solution.py:23
  34.6 3.3 collective-permute-start.5
  37.9 3.8 %collective-permute-done.2 = f32[512,128]{0,1:T(8,128)S(1)} collective-permute-done((f32[512,128]{0,1:T(8,128)S(1)}, f32[512,128]{0,1:T(8,128)S(1)}, u32[]{:S(2)}, u32[]{:S(2)}) %collective-permute-start.2) | collective-permute-done | bytes 262176 | tf_op jit(solution)/shard_map/ppermute | solution.py:23
  42.6 3.5 collective-permute-start.6
  46.1 3.2 collective-permute-done.3
  55.1 2.4 gather_fusion
  57.6 1.9 copy.38
  59.4 12.5 %all-gather.5.cloned.1.call-done = f32[512,4096]{0,1:T(8,128)} async-done(((f32[512,128]{0,1:T(8,128)}), f32[512,4096]{0,1:T(8,128)}) %all-gather.5.cloned.1.call-update) | async-done | bytes 8388624 | tf_op jit(solution)/shard_map/all_gather | solution.py:100
  71.9 16.6 %convolution_multiply_fusion = f32[512,128]{1,0:T(8,128)} fusion(f32[512,128]{1,0:T(8,128)S(1)} %reshape.240, f32[512,4096]{0,1:T(8,128)} %all-gather.5.cloned.1.call-done, f32[4096,128]{1,0:T(8,128)} %bitcast.108), kind=kOutput, calls=%fused_computation.8 | convolution fusion | flops 3221291008 | bytes 11010048 | tf_op jit(solution)/shard_map/dot_general | solution.py:99
  90.4 0.9 reshape.244
  92.2 60.3 %all-gather.7.cloned.1.call-done = f32[512,4096]{1,0:T(8,128)} async-done(((f32[512,128]{1,0:T(8,128)}), f32[512,4096]{1,0:T(8,128)}) %all-gather.7.cloned.1.call-update) | async-done | bytes 8388624 | tf_op jit(solution)/shard_map/all_gather | solution.py:105
  152.6 3.1 dynamic-slice_select_fusion
  155.8 39.8 %all-gather.9.cloned.1.call-done = f32[4096,128]{0,1:T(8,128)} async-done(((f32[512,128]{0,1:T(8,128)}), f32[4096,128]{0,1:T(8,128)}) %all-gather.9.cloned.1.call-update) | async-done | bytes 2097168 | tf_op jit(solution)/shard_map/all_gather | solution.py:97
  195.6 9.3 %fusion.31 = f32[512,128]{1,0:T(8,128)S(1)} fusion(f32[512,4096]{1,0:T(8,128)} %all-gather.7.cloned.1.call-done, f32[4096,128]{0,1:T(8,128)} %all-gather.9.cloned.1.call-done), kind=kOutput, calls=%fused_computation.64 | convolution fusion | flops 3221225472 | bytes 10747904 | tf_op jit(solution)/shard_map/dot_general | solution.py:106
  205.0 49.6 %all-gather.11.cloned.1.call-done = f32[512,4096]{0,1:T(8,128)} async-done(((f32[512,128]{0,1:T(8,128)}), f32[512,4096]{0,1:T(8,128)}) %all-gather.11.cloned.1.call-update) | async-done | bytes 8388624 | tf_op jit(solution)/shard_map/all_gather | solution.py:113
  254.5 83.7 %all-reduce.2.cloned.1.call-done = f32[128,4096]{1,0:T(8,128)} async-done(((f32[128,4096]{1,0:T(8,128)}), f32[128,4096]{1,0:T(8,128)}) %all-reduce.2.cloned.1.call-update) | async-done | bytes 2097168 | tf_op jit(solution)/shard_map/psum | solution.py:34
  338.3 16.0 %fusion = f32[512,128]{1,0:T(8,128)S(1)} fusion(f32[512,128]{1,0:T(8,128)S(1)} %reshape.240, f32[512,128]{1,0:T(8,128)S(1)} %fusion.31, f32[512,4096]{0,1:T(8,128)} %all-gather.11.cloned.1.call-done, f32[128,4096]{1,0:T(8,128)} %all-reduce.2.cloned.1.call-done), kind=kOutput, calls=%fused_computation.7 | convolution fusion | flops 3221356544 | bytes 11272192 | tf_op jit(solution)/shard_map/dot_general | solution.py:112
  355.5 0.8 fusion.7
  (61 shorter events, 11.6 us)
Async XLA Ops:
  6.5 4.4 %copy-start = (f32[1,16,4096]{2,1,0:T(8,128)S(1)}, f32[1,16,4096]{2,1,0:T(8,128)}, u32[]{:S(2)}) copy-start(f32[1,16,4096]{2,1,0:T(8,128)} %param.14) | copy-start | bytes 786436
  6.5 65.4 %all-gather.5.cloned.1.call-start = ((), (), s32[]{:S(2)}) async-start(), calls=%async_computation | async-start | bytes 8650752 | tf_op jit(solution)/shard_map/all_gather | solution.py:100
  7.7 4.1 %copy-start.2 = (s32[1,16]{1,0:T(1,128)S(1)}, s32[1,16]{1,0:T(1,128)}, u32[]{:S(2)}) copy-start(s32[1,16]{1,0:T(1,128)} %param.15) | copy-start | bytes 196
  10.9 30.8 %copy-start.4 = (s32[1,16]{1,0:T(1,128)S(1)}, s32[1,16]{1,0:T(1,128)}, u32[]{:S(2)}) copy-start(s32[1,16]{1,0:T(1,128)} %param.20) | copy-start | bytes 196
  10.9 141.7 %all-gather.7.cloned.1.call-start = ((), (), s32[]{:S(2)}) async-start(), calls=%async_computation.1 | async-start | bytes 8650752 | tf_op jit(solution)/shard_map/all_gather | solution.py:105
  13.0 12.2 %collective-permute-start = (f32[512,128]{0,1:T(8,128)S(1)}, f32[512,128]{0,1:T(8,128)S(1)}, u32[]{:S(2)}, u32[]{:S(2)}) collective-permute-start(f32[512,128]{0,1:T(8,128)S(1)} %reshape.242), channel_id=1, source_target_pairs={{0,32},{32,64},{64,96},{96,128},{128,160},{160,192},{192,224},{224... | collective-permute-start | bytes 786440 | tf_op jit(solution)/shard_map/ppermute | solution.py:23
  25.2 8.7 %collective-permute-start.1 = (f32[512,128]{0,1:T(8,128)S(1)}, f32[512,128]{0,1:T(8,128)S(1)}, u32[]{:S(2)}, u32[]{:S(2)}) collective-permute-start(f32[512,128]{0,1:T(8,128)S(1)} %collective-permute-done), channel_id=1, source_target_pairs={{0,32},{32,64},{64,96},{96,128},{128,160},{160,192},{192,224},{224... | collective-permute-start | bytes 786440 | tf_op jit(solution)/shard_map/ppermute | solution.py:23
  25.2 9.4 %collective-permute-start.4 = (f32[512,128]{0,1:T(8,128)S(1)}, f32[512,128]{0,1:T(8,128)S(1)}, u32[]{:S(2)}, u32[]{:S(2)}) collective-permute-start(f32[512,128]{0,1:T(8,128)S(1)} %reshape.242), channel_id=1, source_target_pairs={{32,0},{64,32},{96,64},{128,96},{160,128},{192,160},{224,192},{0,2... | collective-permute-start | bytes 786440 | tf_op jit(solution)/shard_map/ppermute | solution.py:25
  33.9 7.8 %collective-permute-start.2 = (f32[512,128]{0,1:T(8,128)S(1)}, f32[512,128]{0,1:T(8,128)S(1)}, u32[]{:S(2)}, u32[]{:S(2)}) collective-permute-start(f32[512,128]{0,1:T(8,128)S(1)} %collective-permute-done.1), channel_id=1, source_target_pairs={{0,32},{32,64},{64,96},{96,128},{128,160},{160,192},{192,224},{224... | collective-permute-start | bytes 786440 | tf_op jit(solution)/shard_map/ppermute | solution.py:23
  34.6 8.0 %collective-permute-start.5 = (f32[512,128]{0,1:T(8,128)S(1)}, f32[512,128]{0,1:T(8,128)S(1)}, u32[]{:S(2)}, u32[]{:S(2)}) collective-permute-start(f32[512,128]{0,1:T(8,128)S(1)} %collective-permute-done.4), channel_id=1, source_target_pairs={{32,0},{64,32},{96,64},{128,96},{160,128},{192,160},{224,192},{0,2... | collective-permute-start | bytes 786440 | tf_op jit(solution)/shard_map/ppermute | solution.py:25
  41.7 7.6 %collective-permute-start.3 = (f32[512,128]{0,1:T(8,128)S(1)}, f32[512,128]{0,1:T(8,128)S(1)}, u32[]{:S(2)}, u32[]{:S(2)}) collective-permute-start(f32[512,128]{0,1:T(8,128)S(1)} %collective-permute-done.2), channel_id=1, source_target_pairs={{0,32},{32,64},{64,96},{96,128},{128,160},{160,192},{192,224},{224... | collective-permute-start | bytes 786440 | tf_op jit(solution)/shard_map/ppermute | solution.py:23
  42.6 11.8 %collective-permute-start.6 = (f32[512,128]{0,1:T(8,128)S(1)}, f32[512,128]{0,1:T(8,128)S(1)}, u32[]{:S(2)}, u32[]{:S(2)}) collective-permute-start(f32[512,128]{0,1:T(8,128)S(1)} %collective-permute-done.5), channel_id=1, source_target_pairs={{32,0},{64,32},{96,64},{128,96},{160,128},{192,160},{224,192},{0,2... | collective-permute-start | bytes 786440 | tf_op jit(solution)/shard_map/ppermute | solution.py:25
  71.9 16.7 %copy-start.1 = (f32[1,16,4096]{2,1,0:T(8,128)S(1)}, f32[1,16,4096]{2,1,0:T(8,128)}, u32[]{:S(2)}) copy-start(f32[1,16,4096]{2,1,0:T(8,128)} %param.17) | copy-start | bytes 786436
  71.9 17.5 %copy-start.3 = (s32[1,16]{1,0:T(1,128)S(1)}, s32[1,16]{1,0:T(1,128)}, u32[]{:S(2)}) copy-start(s32[1,16]{1,0:T(1,128)} %param.18) | copy-start | bytes 196
  88.5 107.1 %all-gather.9.cloned.1.call-start = ((), (), s32[]{:S(2)}) async-start(), calls=%async_computation.2 | async-start | bytes 2359296 | tf_op jit(solution)/shard_map/all_gather | solution.py:97
  91.4 163.2 %all-gather.11.cloned.1.call-start = ((), (), s32[]{:S(2)}) async-start(), calls=%async_computation.3 | async-start | bytes 8650752 | tf_op jit(solution)/shard_map/all_gather | solution.py:113
  91.9 246.3 %all-reduce.2.cloned.1.call-start = ((), (), s32[]{:S(2)}) async-start(), calls=%async_computation.4 | async-start | bytes 4194304 | tf_op jit(solution)/shard_map/psum | solution.py:34
Sparse Core Ops, SparseCore 0:
  11.0 60.8 all-gather.4
  88.6 63.8 all-gather.6
  154.4 41.1 all-gather.8
  198.0 56.4 all-gather.10
  256.7 81.4 all-reduce.1
